TPU v7x, 128 devices: a whole 4x4x4 slice. The times are simulated.
128 devices in a mesh: dp: 32 (over x, z, core), rep: 4 (over y).
Axes of the slice: x: 4, y: 4, z: 4, core: 2. Of those that a mesh axis runs over, the one named last changes fastest.
Arguments:
- cross_in: bfloat16 [65536, 3456], P(('dp', 'rep')), may hold values from -24 to 24
- cotangent: bfloat16 [65536, 3456], P(('dp', 'rep')), may hold values from -24 to 24
- weight_down: bfloat16 [3456, 512], replicated, may hold values from -0.109375 to 0.109375
- weight_up: bfloat16 [512, 3456], replicated, may hold values from -0.25 to 0.25
- cross_bias: float32 [3456], replicated, may hold values from -3 to 3
- row_place: int32 [65536, 26], P(('dp', 'rep')), may hold values from 0 to 66559, as said below
- frequent_table: float32 [1024, 128], replicated, may hold values from -0.6 to 0.6
- frequent_accum: float32 [1024], replicated, may hold values from 416 to 106496
- shard_table: float32 [65536, 128], P('dp'), may hold values from -0.6 to 0.6
- shard_accum: float32 [65536], P('dp'), may hold values from 0.01 to 1
Outputs:
- new_frequent: float32 [1024, 128], replicated
- new_frequent_accum: float32 [1024], replicated
- new_shard: float32 [65536, 128], P('dp')
- new_shard_accum: float32 [65536], P('dp')
- grad_up: float32 [512, 3456], P(('dp', 'rep'))
- grad_down: float32 [3456, 512], P(('dp', 'rep'))
- grad_bias: float32 [3456], P(('dp', 'rep'))
Inputs may be any that keep to these rules, and one draw needn't show every extreme that they name: `row_place`: within the rows of one device (aligned blocks of 512 samples), at most 208 entries name rows of any one owner, and in every block some owner is named by exactly 208 entries; every owner is named at least once in every block.
All inputs are finite; a program needn't handle non-finite values.
Results may differ from a plain program's by a relative error of at most 0.0013.
The roundings to bfloat16 on the way count: a program that leaves them out, or rounds other values in their place, can miss the bound.
Values sent between devices are 32-bit elements; how exact they have to be, the bound alone decides.
A program may use at most 192 MiB of HBM per device.

v0:
```python
import jax
import jax.numpy as jnp
from jax import lax
from jax.sharding import PartitionSpec as P

learn_rate = 0.05
eps_ada = 1e-08


def row_adagrad(table, accum, grad):
    accum_new = accum + jnp.mean(grad * grad, axis=1)
    return (table - learn_rate * grad / (jnp.sqrt(accum_new)[:, None] + eps_ada), accum_new)


def body(
    cross_in,
    cotangent,
    weight_down,
    weight_up,
    cross_bias,
    row_place,
    frequent_table,
    frequent_accum,
    shard_table,
    shard_accum,
):
    emb_width = frequent_table.shape[1]
    num_tables = row_place.shape[1]
    local_rows = cross_in.shape[0]
    f_count = frequent_table.shape[0]
    owned_rows = shard_table.shape[0]
    hidden = jnp.dot(cross_in, weight_down, preferred_element_type=jnp.float32).astype(jnp.bfloat16)
    scaled = jnp.dot(hidden, weight_up, preferred_element_type=jnp.float32) + cross_bias
    cot_wide = cotangent.astype(jnp.float32)
    inner = cot_wide * cross_in.astype(jnp.float32)
    inner_half = inner.astype(jnp.bfloat16)
    back_low = lax.dot_general(
        inner_half, weight_up, (((1,), (1,)), ((), ())), preferred_element_type=jnp.float32
    ).astype(jnp.bfloat16)
    back_in = cot_wide * (scaled + 1.0) + lax.dot_general(
        back_low, weight_down, (((1,), (1,)), ((), ())), preferred_element_type=jnp.float32
    )
    local_up = lax.dot_general(
        hidden, inner_half, (((0,), (0,)), ((), ())), preferred_element_type=jnp.float32
    )
    local_down = lax.dot_general(
        cross_in, back_low, (((0,), (0,)), ((), ())), preferred_element_type=jnp.float32
    )
    local_bias = jnp.sum(inner, axis=0)
    grad_up, grad_down, grad_bias = (
        lax.psum_scatter(local_up, ("dp", "rep"), scatter_dimension=0, tiled=True),
        lax.psum_scatter(local_down, ("dp", "rep"), scatter_dimension=0, tiled=True),
        lax.psum_scatter(local_bias, ("dp", "rep"), scatter_dimension=0, tiled=True),
    )
    values = back_in[:, emb_width:].reshape(local_rows * num_tables, emb_width)
    places = row_place.reshape(-1)
    is_frequent = places < f_count
    freq_grad = jax.ops.segment_sum(values, jnp.where(is_frequent, places, f_count), f_count + 1)[
        :f_count
    ]
    shards = lax.axis_size("dp")
    capacity = local_rows * num_tables // (2 * shards)
    owners = jnp.where(is_frequent, shards, (places - f_count) // owned_rows)
    owner_row = jnp.where(is_frequent, 0, (places - f_count) % owned_rows)
    sorted_order = jnp.argsort(owners, stable=True)
    sorted_owner = owners[sorted_order]
    counts = jnp.sum((owners[:, None] == jnp.arange(shards + 1)[None, :]).astype(jnp.int32), axis=0)
    starts = jnp.cumsum(counts) - counts
    slot_pos = jnp.arange(owners.shape[0]) - starts[sorted_owner]
    target = jnp.where(sorted_owner < shards, sorted_owner * capacity + slot_pos, shards * capacity)
    bucket = (
        jnp.zeros((shards * capacity + 1, emb_width), jnp.float32)
        .at[target]
        .set(values[sorted_order])
    )
    bucket = bucket[: shards * capacity].reshape(shards, capacity, emb_width)
    bucket_rows = (
        jnp.zeros((shards * capacity + 1,), jnp.int32).at[target].set(owner_row[sorted_order])
    )
    bucket_rows = bucket_rows[: shards * capacity].reshape(shards, capacity)
    arrived, arrived_rows = (
        lax.all_to_all(bucket, "dp", split_axis=0, concat_axis=0, tiled=True),
        lax.all_to_all(bucket_rows, "dp", split_axis=0, concat_axis=0, tiled=True),
    )
    shard_grad = jax.ops.segment_sum(
        arrived.reshape(-1, emb_width), arrived_rows.reshape(-1), owned_rows
    )
    shard_grad = lax.psum(shard_grad, "rep")
    new_shard, new_shard_accum = row_adagrad(shard_table, shard_accum, shard_grad)
    freq_total = lax.psum(freq_grad, ("dp", "rep"))
    new_frequent, new_frequent_accum = row_adagrad(frequent_table, frequent_accum, freq_total)
    return (
        new_frequent,
        new_frequent_accum,
        new_shard,
        new_shard_accum,
        grad_up,
        grad_down,
        grad_bias,
    )


def solution(mesh):
    in_specs = (
        P(("dp", "rep"), None),
        P(("dp", "rep"), None),
        P(),
        P(),
        P(),
        P(("dp", "rep"), None),
        P(),
        P(),
        P("dp", None),
        P("dp"),
    )
    out_specs = (
        P(),
        P(),
        P("dp", None),
        P("dp"),
        P(("dp", "rep"), None),
        P(("dp", "rep"), None),
        P(("dp", "rep")),
    )
    return jax.shard_map(body, mesh=mesh, in_specs=in_specs, out_specs=out_specs, check_vma=False)
```

profile of v0, /device:TPU:1, one launch (start us, length us, event | category | flops | bytes accessed | tf_op | source)
XLA Modules:
  0.0 876.3 jit_solution(13880018079292635862)
XLA Ops:
  7.2 1.6 broadcast_add_fusion
  9.7 1.7 copy.31
  11.3 1.8 sub.33
  14.9 1.5 fusion.18
  18.1 1.4 reduce-window.9
  22.4 9.1 %sort.17 = (s32[13312]{0:T(1024)}, s32[13312]{0:T(1024)}) sort(s32[13312]{0:T(1024)} %copy-done.2, s32[13312]{0:T(1024)} %iota.12), dimensions={0}, to_apply=%region_3.0 | sort | flops 186368 | bytes 212992 | tf_op jit(solution)/shard_map/jit(argsort)/sort | solution.py:65
  31.5 1.4 fusion.19
  32.9 121.2 %gather_fusion = s32[13312]{0:T(1024)} fusion(s32[13312]{0:T(1024)} %copy-done.2, s32[13312]{0:T(1024)} %fusion.19), kind=kCustom, calls=%fused_computation | custom fusion | bytes 159744 | tf_op jit(solution)/shard_map/gather | solution.py:66
  154.1 5.3 compare_select_fusion.3
  159.4 4.2 compare_reduce_fusion.25
  163.7 16.6 %select_select_fusion = s32[13312]{0:T(1024)S(1)} fusion(pred[13312]{0:T(1024)(128)(4,1)S(1)} %get-tuple-element.62, pred[13312]{0:T(1024)(128)(4,1)S(1)} %get-tuple-element.61, pred[13312]{0:T(1024)(128)(4,1)S(1)} %get-tuple-element.60, pred[13312]{0:T(1024)(128)(4,1)S(1)} %get-tuple-element.59, pred[13312]{0:T(1024)(128)(4,1)S(1)} %get-tuple-element.58, ...), kind=kLoop, calls=%fused_computation.77 | loop fusion | flops 346112 | bytes 452712 | tf_op jit(solution)/shard_map/gather | solution.py:69
  180.3 1.6 compare_select_fusion
  181.8 120.7 %gather_fusion.1 = s32[13312]{0:T(1024)} fusion(s32[13312]{0:T(1024)} %get-tuple-element.72, s32[13312]{0:T(1024)} %fusion.19), kind=kCustom, calls=%fused_computation.1 | custom fusion | bytes 159744 | tf_op jit(solution)/shard_map/gather | solution.py:78
  302.6 49.8 %scatter_custom_fusion.1 = s32[6657]{0:T(1024)} fusion(s32[13312]{0:T(1024)} %bitcast.62, s32[13312]{0:T(1024)} %gather_fusion.1, s32[]{:T(128)} %constant.29.clone.1), kind=kCustom, calls=%fused_computation.83 | custom fusion | bytes 27140 | tf_op jit(solution)/shard_map/scatter | solution.py:78
  352.4 1.5 all_to_all.9
  353.9 9.8 %all-to-all-start = ((s32[32,1,208]{2,1,0:T(1,128)}), s32[32,1,208]{2,1,0:T(1,128)}, u32[]{:S(2)}, u32[]{:S(2)}) async-start(s32[32,1,208]{2,1,0:T(1,128)} %all_to_all.9), calls=%async_computation | async-start | bytes 65536 | tf_op jit(solution)/shard_map/all_to_all | solution.py:83
  363.7 2.6 convert_element_type.18
  367.9 2.0 convolution_convert_fusion
  369.9 2.1 fusion.10
  372.1 2.1 fusion.26
  374.3 2.1 fusion.27
  376.4 3.3 slice_add_fusion
  379.7 7.8 reshape.231
  387.5 108.6 %scatter_custom_fusion.2 = f32[6657,128]{1,0:T(8,128)S(1)} fusion(s32[13312]{0:T(1024)} %bitcast.63, f32[13312,128]{1,0:T(8,128)} %reshape.231, s32[13312]{0:T(1024)} %fusion.19, f32[]{:T(128)} %constant.21.clone.1), kind=kCustom, calls=%fused_computation.12 | custom fusion | bytes 3408896 | tf_op jit(solution)/shard_map/scatter | solution.py:74
  496.1 2.1 slice.62
  498.2 7.8 all-to-all-start.1
  506.1 1.7 copy.29
  507.8 1.8 reshape.157
  509.6 1.5 compare_select_fusion.2
  511.1 72.4 %scatter_custom_fusion = f32[1025,128]{1,0:T(8,128)} fusion(s32[13312]{0:T(1024)} %bitcast.64, f32[13312,128]{1,0:T(8,128)} %reshape.231, f32[]{:T(128)} %constant.21.clone.1), kind=kCustom, calls=%fused_computation.33 | custom fusion | flops 1703936 | bytes 525312 | tf_op jit(solution)/shard_map/scatter-add | solution.py:58
  583.4 1.9 slice.60
  585.3 1.4 reduce.27
  586.8 1.5 reshape.253
  588.2 41.0 %scatter_custom_fusion.3 = f32[2048,128]{1,0:T(8,128)} fusion(s32[6656]{0:T(1024)} %reshape.253, f32[6656,128]{1,0:T(8,128)} %bitcast.40, f32[]{:T(128)} %constant.21.clone.1), kind=kCustom, calls=%fused_computation.26 | custom fusion | flops 851968 | bytes 1049088 | tf_op jit(solution)/shard_map/scatter-add | solution.py:85
  629.4 6.2 convolution_bitcast_fusion
  635.6 5.1 fusion.6
  640.7 4.2 fusion.3
  644.8 67.5 %all-reduce.2 = f32[3456]{0:T(1024)} all-reduce(f32[3456]{0:T(1024)S(1)} %fusion.3), channel_id=4, replica_groups=mesh['dp'=32,'rep'=4] {'dp','rep'}, use_global_device_ids=true, to_apply=%region_14.15.clone | all-reduce | flops 3456 | bytes 27648
  712.3 1.3 dynamic-slice.2
  713.6 1.6 multiply_reduce_fusion
  715.2 1.3 sqrt_add_fusion
  716.5 3.0 divide_subtract_fusion
  719.4 140.0 %all-reduce.9.cloned.1.call-done = (f32[1024,128]{1,0:T(8,128)}, f32[512,3456]{1,0:T(8,128)}, f32[3456,512]{0,1:T(8,128)}) async-done(((f32[1024,128]{1,0:T(8,128)}, f32[512,3456]{1,0:T(8,128)}, f32[3456,512]{0,1:T(8,128)}), (f32[1024,128]{1,0:T(8,128)}, f32[512,3456]{1,0:T(8,128)}, f32[3456,512]{0,1:T(8,128)})) %all-reduce.9.cloned.1.call-update) | async-done | bytes 14680080 | tf_op jit(solution)/shard_map/psum | solution.py:90
  860.7 1.9 constant_dynamic-slice_fusion
  862.6 1.7 copy.33
  864.3 1.3 sqrt_add_fusion.1
  865.5 2.2 divide_subtract_fusion.1
  867.7 1.5 constant_dynamic-slice_fusion.1
  (45 shorter events, 10.3 us)
Async XLA Ops:
  7.2 362.8 %copy-start = (bf16[512,3456]{1,0:T(8,128)(2,1)S(1)}, bf16[512,3456]{1,0:T(8,128)(2,1)}, u32[]{:S(2)}) copy-start(bf16[512,3456]{1,0:T(8,128)(2,1)} %param.13) | copy-start | bytes 10616836
  16.4 0.6 copy-start.2
  353.9 144.3 %all-to-all-start = ((s32[32,1,208]{2,1,0:T(1,128)}), s32[32,1,208]{2,1,0:T(1,128)}, u32[]{:S(2)}, u32[]{:S(2)}) async-start(s32[32,1,208]{2,1,0:T(1,128)} %all_to_all.9), calls=%async_computation | async-start | bytes 65536 | tf_op jit(solution)/shard_map/all_to_all | solution.py:83
  363.7 3.1 copy-start.3
  363.7 4.1 copy-start.7
  367.9 2.1 copy-start.5
  369.9 2.1 copy-start.9
  372.1 4.3 copy-start.11
  372.1 2.2 copy-start.8
  374.3 2.1 copy-start.12
  498.2 131.1 %copy-start.4 = (bf16[512,3456]{1,0:T(8,128)(2,1)S(1)}, bf16[512,3456]{1,0:T(8,128)(2,1)}, u32[]{:S(2)}) copy-start(bf16[512,3456]{1,0:T(8,128)(2,1)} %param.10) | copy-start | bytes 10616836
  498.2 90.0 %all-to-all-start.1 = ((f32[32,208,128]{2,1,0:T(8,128)}), f32[32,208,128]{2,1,0:T(8,128)}, u32[]{:S(2)}, u32[]{:S(2)}) async-start(f32[32,208,128]{2,1,0:T(8,128)} %bitcast.56), calls=%async_computation.1 | async-start | bytes 6815744 | tf_op jit(solution)/shard_map/all_to_all | solution.py:82
  506.1 207.5 %all-reduce.7.cloned.1.call-start = ((), (), s32[]{:S(2)}) async-start(), calls=%async_computation.2 | async-start | bytes 2097152 | tf_op jit(solution)/shard_map/psum | solution.py:88
  629.3 230.1 %all-reduce.9.cloned.1.call-start = ((), (), s32[]{:S(2)}) async-start(), calls=%async_computation.3 | async-start | bytes 29360128 | tf_op jit(solution)/shard_map/psum | solution.py:90
  629.3 6.2 copy-start.6
  629.4 6.2 copy-start.10
  640.7 228.6 %copy-start.1 = (bf16[512,3456]{1,0:T(8,128)(2,1)S(1)}, bf16[512,3456]{1,0:T(8,128)(2,1)}, u32[]{:S(2)}) copy-start(bf16[512,3456]{1,0:T(8,128)(2,1)} %param.13) | copy-start | bytes 10616836
Sparse Core Ops, SparseCore 0:
  629.4 46.4 all-reduce.6
  683.0 176.4 all-reduce.8
where the time goes:
time: 884 us; the launch traced here: 876 us
  local copies, waits for them, and re-layouts  435 us (49%)
  other arithmetic  182 us (21%)
  waiting for transfers between devices  140 us (16%)
  blocking collectives  67.5 us (8%)
  matrix products  19.6 us (2%)
  starting transfers between devices  17.8 us (2%)
  between operations  14.5 us (2%)
    psum x1, waiting for transfers between devices, body(): freq_total = lax.psum(freq_grad, ('dp', 'rep'))  140 us
    gather x1, local copies, waits for them, and re-layouts, body(): sorted_owner = owners[sorted_order]  121 us
    gather x1, local copies, waits for them, and re-layouts, body(): owner_row[sorted_order]  121 us
    scatter x1, local copies, waits for them, and re-layouts, body(): bucket = jnp.zeros((shards * capacity + 1, emb_width), jnp.float32).at[ta...  109 us
    scatter-add x1, other arithmetic, body(): jax.ops.segment_sum(values, jnp.where(is_frequent, places, f_count), f_co...  72.4 us
    unnamed x1, blocking collectives  67.5 us
    scatter x1, local copies, waits for them, and re-layouts, body(): jnp.zeros((shards * capacity + 1,), jnp.int32).at[target]  49.8 us
    scatter-add x1, other arithmetic, body(): jax.ops.segment_sum(arrived.reshape(-1, emb_width), arrived_rows.reshape(...  41 us
  transfers between devices with their start and end apart: 4, of which 1 were waited for; matrix products, arithmetic and copies ran while one was open for 27% of the time, Pallas kernels for 0%

commit v1 on v0

--- a/solution.py
+++ b/solution.py
@@ -87,7 +87,7 @@
     )
     shard_grad = lax.psum(shard_grad, "rep")
     new_shard, new_shard_accum = row_adagrad(shard_table, shard_accum, shard_grad)
-    freq_total = lax.psum(freq_grad, ("dp", "rep"))
+    freq_total = lax.psum(lax.psum(freq_grad, "rep"), "dp")
     new_frequent, new_frequent_accum = row_adagrad(frequent_table, frequent_accum, freq_total)
     return (
         new_frequent,

time: 884 us -> 987 us (1.12)
  waiting for transfers between devices: 140 us -> 243 us
    unnamed x2 -> x4, waiting for transfers between devices: 0.03 us -> 173 us
    psum x2, waiting for transfers between devices: 140 us -> 69.7 us  [body(): freq_total = lax.psum(lax.psum(freq_grad, 'rep'), 'dp')]
  transfers between devices with their start and end apart: 4 -> 5, of which waited for: 1 -> 3; matrix products, arithmetic and copies ran while one was open for 27% -> 25% of each run, Pallas kernels for 0% -> 0%
where the time goes in v1:
time: 987 us; the launch traced here: 979 us
  local copies, waits for them, and re-layouts  435 us (44%)
  waiting for transfers between devices  243 us (25%)
  other arithmetic  182 us (18%)
  blocking collectives  65.6 us (7%)
  matrix products  21.6 us (2%)
  starting transfers between devices  17.8 us (2%)
  between operations  14.2 us (1%)
    unnamed x4, waiting for transfers between devices  173 us
    gather x1, local copies, waits for them, and re-layouts, body(): sorted_owner = owners[sorted_order]  121 us
    gather x1, local copies, waits for them, and re-layouts, body(): owner_row[sorted_order]  121 us
    scatter x1, local copies, waits for them, and re-layouts, body(): bucket = jnp.zeros((shards * capacity + 1, emb_width), jnp.float32).at[ta...  109 us
    scatter-add x1, other arithmetic, body(): jax.ops.segment_sum(values, jnp.where(is_frequent, places, f_count), f_co...  72.4 us
    psum x2, waiting for transfers between devices, body(): freq_total = lax.psum(lax.psum(freq_grad, 'rep'), 'dp')  69.7 us
    unnamed x1, blocking collectives  65.6 us
    scatter x1, local copies, waits for them, and re-layouts, body(): jnp.zeros((shards * capacity + 1,), jnp.int32).at[target]  49.8 us
  transfers between devices with their start and end apart: 5, of which 3 were waited for; matrix products, arithmetic and copies ran while one was open for 25% of the time, Pallas kernels for 0%

profile of v1, /device:TPU:1, one launch (start us, length us, event | category | flops | bytes accessed | tf_op | source)
XLA Modules:
  0.0 979.0 jit_solution(15853619704225845333)
XLA Ops:
  7.2 1.6 broadcast_add_fusion
  9.7 1.7 copy.31
  11.3 1.8 sub.33
  14.9 1.5 fusion.18
  18.1 1.4 reduce-window.9
  22.4 9.1 sort.17
  31.5 1.4 fusion.19
  32.9 121.2 %gather_fusion = s32[13312]{0:T(1024)} fusion(s32[13312]{0:T(1024)} %copy-done.2, s32[13312]{0:T(1024)} %fusion.19), kind=kCustom, calls=%fused_computation | custom fusion | bytes 159744 | tf_op jit(solution)/shard_map/gather | solution.py:66
  154.1 5.3 compare_select_fusion.3
  159.4 4.2 compare_reduce_fusion.25
  163.7 16.6 %select_select_fusion = s32[13312]{0:T(1024)S(1)} fusion(pred[13312]{0:T(1024)(128)(4,1)S(1)} %get-tuple-element.62, pred[13312]{0:T(1024)(128)(4,1)S(1)} %get-tuple-element.61, pred[13312]{0:T(1024)(128)(4,1)S(1)} %get-tuple-element.60, pred[13312]{0:T(1024)(128)(4,1)S(1)} %get-tuple-element.59, pred[13312]{0:T(1024)(128)(4,1)S(1)} %get-tuple-element.58, ...), kind=kLoop, calls=%fused_computation.77 | loop fusion | flops 346112 | bytes 452712 | tf_op jit(solution)/shard_map/gather | solution.py:69
  180.3 1.6 compare_select_fusion
  181.8 120.7 %gather_fusion.1 = s32[13312]{0:T(1024)} fusion(s32[13312]{0:T(1024)} %get-tuple-element.73, s32[13312]{0:T(1024)} %fusion.19), kind=kCustom, calls=%fused_computation.1 | custom fusion | bytes 159744 | tf_op jit(solution)/shard_map/gather | solution.py:78
  302.6 49.8 %scatter_custom_fusion.1 = s32[6657]{0:T(1024)} fusion(s32[13312]{0:T(1024)} %bitcast.62, s32[13312]{0:T(1024)} %gather_fusion.1, s32[]{:T(128)} %constant.29.clone.1), kind=kCustom, calls=%fused_computation.83 | custom fusion | bytes 27140 | tf_op jit(solution)/shard_map/scatter | solution.py:78
  352.4 1.5 all_to_all.9
  353.9 9.8 %all-to-all-start = ((s32[32,1,208]{2,1,0:T(1,128)}), s32[32,1,208]{2,1,0:T(1,128)}, u32[]{:S(2)}, u32[]{:S(2)}) async-start(s32[32,1,208]{2,1,0:T(1,128)} %all_to_all.9), calls=%async_computation | async-start | bytes 65536 | tf_op jit(solution)/shard_map/all_to_all | solution.py:83
  363.7 2.6 convert_element_type.18
  367.9 2.0 convolution_convert_fusion
  369.9 2.1 fusion.10
  372.1 2.1 fusion.26
  374.3 2.1 fusion.27
  376.4 3.3 slice_add_fusion
  379.7 7.8 reshape.231
  387.5 108.6 %scatter_custom_fusion.2 = f32[6657,128]{1,0:T(8,128)S(1)} fusion(s32[13312]{0:T(1024)} %bitcast.63, f32[13312,128]{1,0:T(8,128)} %reshape.231, s32[13312]{0:T(1024)} %fusion.19, f32[]{:T(128)} %constant.21.clone.1), kind=kCustom, calls=%fused_computation.12 | custom fusion | bytes 3408896 | tf_op jit(solution)/shard_map/scatter | solution.py:74
  496.1 2.1 slice.62
  498.2 7.8 all-to-all-start.1
  506.1 1.7 copy.29
  507.8 1.8 reshape.157
  509.6 1.5 compare_select_fusion.2
  511.1 72.4 %scatter_custom_fusion = f32[1025,128]{1,0:T(8,128)} fusion(s32[13312]{0:T(1024)} %bitcast.64, f32[13312,128]{1,0:T(8,128)} %reshape.231, f32[]{:T(128)} %constant.21.clone.1), kind=kCustom, calls=%fused_computation.33 | custom fusion | flops 1703936 | bytes 525312 | tf_op jit(solution)/shard_map/scatter-add | solution.py:58
  583.4 1.9 slice.60
  585.3 1.4 reduce.27
  586.8 1.5 reshape.253
  588.2 41.0 %scatter_custom_fusion.3 = f32[2048,128]{1,0:T(8,128)} fusion(s32[6656]{0:T(1024)} %reshape.253, f32[6656,128]{1,0:T(8,128)} %bitcast.40, f32[]{:T(128)} %constant.21.clone.1), kind=kCustom, calls=%fused_computation.26 | custom fusion | flops 851968 | bytes 1049088 | tf_op jit(solution)/shard_map/scatter-add | solution.py:85
  629.3 7.2 fusion.6
  636.5 45.3 %all-reduce.13.cloned.1.call-done = (f32[1024,128]{1,0:T(8,128)}, f32[2048,128]{1,0:T(8,128)}) async-done(((f32[1024,128]{1,0:T(8,128)}, f32[2048,128]{1,0:T(8,128)}), (f32[1024,128]{1,0:T(8,128)}, f32[2048,128]{1,0:T(8,128)})) %all-reduce.13.cloned.1.call-update) | async-done | bytes 1572880 | tf_op jit(solution)/shard_map/psum | solution.py:90
  681.9 6.1 convolution_bitcast_fusion
  688.1 4.2 fusion.3
  692.2 65.6 %all-reduce.2 = f32[3456]{0:T(1024)} all-reduce(f32[3456]{0:T(1024)S(1)} %fusion.3), channel_id=4, replica_groups=mesh['dp'=32,'rep'=4] {'dp','rep'}, use_global_device_ids=true, to_apply=%region_15.16.clone | all-reduce | flops 3456 | bytes 27648
  759.1 1.6 multiply_reduce_fusion
  760.7 1.3 sqrt_add_fusion
  762.0 2.9 divide_subtract_fusion
  764.8 24.4 %all-reduce.9.cloned.1.call-done = f32[1024,128]{1,0:T(8,128)} async-done(((f32[1024,128]{1,0:T(8,128)}), f32[1024,128]{1,0:T(8,128)}) %all-reduce.9.cloned.1.call-update) | async-done | bytes 524304 | tf_op jit(solution)/shard_map/psum | solution.py:90
  791.8 2.2 divide_subtract_fusion.1
  794.0 173.2 %all-reduce.11.cloned.1.call-done = (f32[512,3456]{1,0:T(8,128)}, f32[3456,512]{0,1:T(8,128)}) async-done(((f32[512,3456]{1,0:T(8,128)}, f32[3456,512]{0,1:T(8,128)}), (f32[512,3456]{1,0:T(8,128)}, f32[3456,512]{0,1:T(8,128)})) %all-reduce.11.cloned.1.call-update) | async-done | bytes 14155792
  967.2 1.9 constant_dynamic-slice_fusion
  969.0 1.7 copy.33
  970.7 1.5 constant_dynamic-slice_fusion.1
  (44 shorter events, 12.9 us)
Async XLA Ops:
  7.2 362.8 %copy-start = (bf16[512,3456]{1,0:T(8,128)(2,1)S(1)}, bf16[512,3456]{1,0:T(8,128)(2,1)}, u32[]{:S(2)}) copy-start(bf16[512,3456]{1,0:T(8,128)(2,1)} %param.13) | copy-start | bytes 10616836
  16.4 0.6 copy-start.2
  353.9 144.3 %all-to-all-start = ((s32[32,1,208]{2,1,0:T(1,128)}), s32[32,1,208]{2,1,0:T(1,128)}, u32[]{:S(2)}, u32[]{:S(2)}) async-start(s32[32,1,208]{2,1,0:T(1,128)} %all_to_all.9), calls=%async_computation | async-start | bytes 65536 | tf_op jit(solution)/shard_map/all_to_all | solution.py:83
  363.7 3.1 copy-start.3
  363.7 4.1 copy-start.6
  367.9 2.1 copy-start.5
  369.9 2.1 copy-start.8
  372.1 4.3 copy-start.9
  372.1 2.2 copy-start.7
  374.3 2.1 copy-start.10
  498.2 131.1 %copy-start.4 = (bf16[512,3456]{1,0:T(8,128)(2,1)S(1)}, bf16[512,3456]{1,0:T(8,128)(2,1)}, u32[]{:S(2)}) copy-start(bf16[512,3456]{1,0:T(8,128)(2,1)} %param.10) | copy-start | bytes 10616836
  498.2 90.0 %all-to-all-start.1 = ((f32[32,208,128]{2,1,0:T(8,128)}), f32[32,208,128]{2,1,0:T(8,128)}, u32[]{:S(2)}, u32[]{:S(2)}) async-start(f32[32,208,128]{2,1,0:T(8,128)} %bitcast.56), calls=%async_computation.1 | async-start | bytes 6815744 | tf_op jit(solution)/shard_map/all_to_all | solution.py:82
  506.1 175.8 %all-reduce.13.cloned.1.call-start = ((), (), s32[]{:S(2)}) async-start(), calls=%async_computation.4 | async-start | bytes 3145728 | tf_op jit(solution)/shard_map/psum | solution.py:90
  629.3 160.0 %all-reduce.9.cloned.1.call-start = ((), (), s32[]{:S(2)}) async-start(), calls=%async_computation.2 | async-start | bytes 1048576 | tf_op jit(solution)/shard_map/psum | solution.py:90
  681.9 285.3 %all-reduce.11.cloned.1.call-start = ((), (), s32[]{:S(2)}) async-start(), calls=%async_computation.3 | async-start | bytes 28311552
  688.0 284.2 %copy-start.1 = (bf16[512,3456]{1,0:T(8,128)(2,1)S(1)}, bf16[512,3456]{1,0:T(8,128)(2,1)}, u32[]{:S(2)}) copy-start(bf16[512,3456]{1,0:T(8,128)(2,1)} %param.13) | copy-start | bytes 10616836
Sparse Core Ops, SparseCore 0:
  629.4 52.4 all-reduce.12
  685.1 104.1 all-reduce.8
  795.2 171.9 all-reduce.10
